TPU v7x, 32 devices: a whole 2x2x4 slice. The times are simulated.
32 devices in a mesh: groups: 2 (over y), tile: 16 (over z, x, core).
Axes of the slice: x: 2, y: 2, z: 4, core: 2. Of those that a mesh axis runs over, the one named last changes fastest.
Arguments:
- fine: bfloat16 [64, 256, 256], P(('groups', 'tile')), parts along dimension 0, may hold values from -12 to 12
- conv_weight: bfloat16 [3, 3, 256, 256], replicated, may hold values from -0.125 to 0.125
- qk_weight: bfloat16 [2, 256, 128], replicated, may hold values from -2 to 2
- v_weight: bfloat16 [256, 128], replicated, may hold values from -0.375 to 0.375
- o_weight: bfloat16 [128, 256], replicated, may hold values from -0.5 to 0.5
- upstream: bfloat16 [4096, 256], P(('groups', 'tile')), parts along dimension 0, may hold values from -6 to 6
Outputs:
- block_out: bfloat16 [4096, 256], P(('groups', 'tile')), parts along dimension 0
- grad_conv: float32 [6, 3, 256, 256], P('groups'), parts along dimension 0
- grad_fine: bfloat16 [64, 256, 256], P(('groups', 'tile')), parts along dimension 0
There are 2 independent parts, one for each index of `groups`. A program takes and returns all parts, laid end to end along the dimension named above; an argument that names none is the same for every part. Nothing has to cross between parts.
All inputs are finite; a program needn't handle non-finite values.
Results may differ from a plain program's by a relative error of at most 0.035.
The roundings to bfloat16 on the way count: a program that leaves them out, or rounds other values in their place, can miss the bound.
Values may be sent and summed in bfloat16 or wider, within the bound.
A program may use at most 64 MiB of HBM per device.

v0:
```python
import math

import jax
import jax.numpy as jnp
from jax import lax
from jax.sharding import PartitionSpec as P

HEADS = 2
HDIM = 64
HD = 128


def shifted(x, axis, by):
    peers = lax.axis_size(axis)
    pairs = [(i, i + by) for i in range(peers) if 0 <= i + by < peers]
    return lax.ppermute(x, axis, pairs)


def head_view(mat):
    return mat.reshape(mat.shape[0], HEADS, HDIM)


def score_block(queries, keys):
    product = jnp.einsum(
        "qhd,khd->hqk", head_view(queries), head_view(keys), preferred_element_type=jnp.float32
    )
    return product * HDIM ** (-0.5)


def dot_back(left, right):
    return lax.dot_general(
        left, right, (((1,), (1,)), ((), ())), preferred_element_type=jnp.float32
    )


def dot_over(left, right):
    return lax.dot_general(
        left, right, (((0,), (0,)), ((), ())), preferred_element_type=jnp.float32
    )


def body(fine, conv_weight, qk_weight, v_weight, o_weight, upstream):
    rows = fine.shape[0] // 2
    cols = fine.shape[1] // 2
    chans = fine.shape[2]
    local = rows * cols
    scale = HDIM ** (-0.5)
    above = shifted(fine[-1:], "tile", 1)
    padded = jnp.pad(jnp.concatenate([above, fine], axis=0), ((0, 0), (1, 0), (0, 0)))
    taps = []
    total = jnp.zeros((local, chans), jnp.float32)
    for a in range(3):
        for b in range(3):
            tap = padded[a : a + 2 * rows : 2, b : b + 2 * cols : 2].reshape(local, chans)
            taps.append(tap)
            total = total + jnp.dot(tap, conv_weight[a, b], preferred_element_type=jnp.float32)
    hidden = total.astype(jnp.bfloat16)
    query = jnp.dot(hidden, qk_weight[0], preferred_element_type=jnp.float32).astype(jnp.bfloat16)
    key_loc = jnp.dot(hidden, qk_weight[1], preferred_element_type=jnp.float32).astype(jnp.bfloat16)
    value_loc = jnp.dot(hidden, v_weight, preferred_element_type=jnp.float32).astype(jnp.bfloat16)
    keys_all, values_all = (
        lax.all_gather(key_loc, "tile", axis=0, tiled=True),
        lax.all_gather(value_loc, "tile", axis=0, tiled=True),
    )
    everyone = keys_all.shape[0]
    block = math.gcd(everyone, 2048)
    steps_total = everyone // block

    def stats_step(index, carry):
        top, summed = carry
        scores = score_block(query, lax.dynamic_slice_in_dim(keys_all, index * block, block, 0))
        new_top = jnp.maximum(top, jnp.max(scores, axis=2))
        summed = summed * jnp.exp(top - new_top) + jnp.sum(
            jnp.exp(scores - new_top[:, :, None]), axis=2
        )
        return (new_top, summed)

    start_top = jnp.full((HEADS, local), -jnp.inf, jnp.float32)
    top, summed = lax.fori_loop(
        0, steps_total, stats_step, (start_top, jnp.zeros((HEADS, local), jnp.float32))
    )
    lse = top + jnp.log(summed)

    def value_step(index, acc):
        scores = score_block(query, lax.dynamic_slice_in_dim(keys_all, index * block, block, 0))
        weights = jnp.exp(scores - lse[:, :, None]).astype(jnp.bfloat16)
        v_part = head_view(lax.dynamic_slice_in_dim(values_all, index * block, block, 0))
        return acc + jnp.einsum("hqk,khd->qhd", weights, v_part, preferred_element_type=jnp.float32)

    mixed = lax.fori_loop(0, steps_total, value_step, jnp.zeros((local, HEADS, HDIM), jnp.float32))
    attended = mixed.reshape(local, HD).astype(jnp.bfloat16)
    block_out = (
        hidden.astype(jnp.float32) + jnp.dot(attended, o_weight, preferred_element_type=jnp.float32)
    ).astype(jnp.bfloat16)
    dattended = dot_back(upstream, o_weight).astype(jnp.bfloat16)
    product = dattended.astype(jnp.float32) * attended.astype(jnp.float32)
    delta = jnp.sum(product.reshape(local, HEADS, HDIM), axis=2).T

    def query_step(index, acc):
        k_part = lax.dynamic_slice_in_dim(keys_all, index * block, block, 0)
        v_part = lax.dynamic_slice_in_dim(values_all, index * block, block, 0)
        prob = jnp.exp(score_block(query, k_part) - lse[:, :, None])
        dprob = jnp.einsum(
            "qhd,khd->hqk",
            head_view(dattended),
            head_view(v_part),
            preferred_element_type=jnp.float32,
        )
        dscore = (prob * (dprob - delta[:, :, None]) * scale).astype(jnp.bfloat16)
        return acc + jnp.einsum(
            "hqk,khd->qhd", dscore, head_view(k_part), preferred_element_type=jnp.float32
        )

    dq_acc = lax.fori_loop(0, steps_total, query_step, jnp.zeros((local, HEADS, HDIM), jnp.float32))
    dquery = dq_acc.reshape(local, HD).astype(jnp.bfloat16)
    lse_all, delta_all = (
        lax.all_gather(lse.T, "tile", axis=0, tiled=True),
        lax.all_gather(delta.T, "tile", axis=0, tiled=True),
    )
    empty = jnp.zeros((local, HEADS, HDIM), jnp.float32)
    q_in = lax.all_gather(query, "tile", axis=0, tiled=True)
    d_in = lax.all_gather(dattended, "tile", axis=0, tiled=True)
    incoming = q_in.shape[0]
    sub = math.gcd(incoming, 2048)

    def inner(index, acc):
        dk_acc, dv_acc = acc
        at = index * sub
        q_part = lax.dynamic_slice_in_dim(q_in, at, sub, 0)
        d_part = lax.dynamic_slice_in_dim(d_in, at, sub, 0)
        l_part = lax.dynamic_slice_in_dim(lse_all, at, sub, 0).T
        e_part = lax.dynamic_slice_in_dim(delta_all, at, sub, 0).T
        prob = jnp.exp(score_block(q_part, key_loc) - l_part[:, :, None])
        dv_acc = dv_acc + jnp.einsum(
            "hqk,qhd->khd",
            prob.astype(jnp.bfloat16),
            head_view(d_part),
            preferred_element_type=jnp.float32,
        )
        dprob = jnp.einsum(
            "qhd,khd->hqk",
            head_view(d_part),
            head_view(value_loc),
            preferred_element_type=jnp.float32,
        )
        dscore = (prob * (dprob - e_part[:, :, None]) * scale).astype(jnp.bfloat16)
        dk_acc = dk_acc + jnp.einsum(
            "hqk,qhd->khd", dscore, head_view(q_part), preferred_element_type=jnp.float32
        )
        return (dk_acc, dv_acc)

    dk_acc, dv_acc = lax.fori_loop(0, incoming // sub, inner, (empty, empty))
    dkeys = dk_acc.reshape(local, HD).astype(jnp.bfloat16)
    dvalues = dv_acc.reshape(local, HD).astype(jnp.bfloat16)
    dhidden = upstream.astype(jnp.float32)
    dhidden = dhidden + dot_back(dquery, qk_weight[0])
    dhidden = dhidden + dot_back(dkeys, qk_weight[1])
    dhidden = dhidden + dot_back(dvalues, v_weight)
    dhidden = dhidden.astype(jnp.bfloat16)
    kernel_rows = []
    dpadded = jnp.zeros((2 * rows + 1, 2 * cols + 1, chans), jnp.float32)
    for a in range(3):
        row_list = []
        for b in range(3):
            row_list.append(dot_over(taps[3 * a + b], dhidden))
            back = dot_back(dhidden, conv_weight[a, b])
            dpadded = dpadded.at[a : a + 2 * rows : 2, b : b + 2 * cols : 2].add(
                back.reshape(rows, cols, chans)
            )
        kernel_rows.append(jnp.stack(row_list))
    kernel_local = jnp.stack(kernel_rows)
    grad_conv = lax.psum(kernel_local, "tile") * (1.0 / math.sqrt(everyone))
    below = shifted(dpadded[0:1, 1:].astype(jnp.bfloat16), "tile", -1).astype(jnp.float32)
    grad_fine = dpadded[1:, 1:]
    grad_fine = grad_fine.at[-1:].add(below)
    return (block_out, grad_conv, grad_fine.astype(jnp.bfloat16))


def solution(mesh):
    return jax.shard_map(
        body,
        mesh=mesh,
        in_specs=(
            P(("groups", "tile"), None, None),
            P(),
            P(),
            P(),
            P(),
            P(("groups", "tile"), None),
        ),
        out_specs=(
            P(("groups", "tile"), None),
            P("groups", None, None, None),
            P(("groups", "tile"), None, None),
        ),
        check_vma=False,
    )
```

profile of v0, /device:TPU:0, one launch (start us, length us, event | category | flops | bytes accessed | tf_op | source)
XLA Modules:
  0.0 278.1 jit_solution(12936537645848103998)
XLA Ops:
  8.2 2.4 collective-permute-start
  11.6 1.1 fusion.26
  16.0 27.5 %all_gather.19 = bf16[2048,128]{0,1:T(8,128)(2,1)S(1)} all-gather(bf16[128,128]{0,1:T(8,128)(2,1)S(1)} %convolution_convert_fusion.3), channel_id=1, replica_groups=mesh['groups'=2,'tile'=16] {'tile'}, dimensions={0}, use_global_device_ids=true | all-gather | bytes 557056 | tf_op jit(solution)/shard_map/all_gather | solution.py:62
  43.4 20.3 %all_gather.20 = bf16[2048,128]{0,1:T(8,128)(2,1)} all-gather(bf16[128,128]{0,1:T(8,128)(2,1)S(1)} %convolution_convert_fusion.4), channel_id=1, replica_groups=mesh['groups'=2,'tile'=16] {'tile'}, dimensions={0}, use_global_device_ids=true | all-gather | bytes 557056 | tf_op jit(solution)/shard_map/all_gather | solution.py:121
  65.0 20.5 %all_gather.18 = bf16[2048,128]{0,1:T(8,128)(2,1)S(1)} all-gather(bf16[128,128]{0,1:T(8,128)(2,1)S(1)} %convolution_convert_fusion.5), channel_id=1, replica_groups=mesh['groups'=2,'tile'=16] {'tile'}, dimensions={0}, use_global_device_ids=true | all-gather | bytes 557056 | tf_op jit(solution)/shard_map/all_gather | solution.py:63
  88.3 20.3 %all_gather.22 = bf16[2048,128]{0,1:T(8,128)(2,1)} all-gather(bf16[128,128]{0,1:T(8,128)(2,1)S(1)} %get-tuple-element.113), channel_id=1, replica_groups=mesh['groups'=2,'tile'=16] {'tile'}, dimensions={0}, use_global_device_ids=true | all-gather | bytes 557056 | tf_op jit(solution)/shard_map/all_gather | solution.py:122
  108.5 20.3 %all_gather.23 = f32[2048,2]{0,1:T(2,128)} all-gather(f32[128,2]{0,1:T(2,128)S(1)} %get-tuple-element.112), channel_id=1, replica_groups=mesh['groups'=2,'tile'=16] {'tile'}, dimensions={0}, use_global_device_ids=true | all-gather | bytes 17408 | tf_op jit(solution)/shard_map/all_gather | solution.py:118
  128.8 2.8 %fusion.14 = bf16[2,64,128]{2,1,0:T(8,128)(2,1)} fusion(bf16[2048,2,64]{0,2,1:T(8,128)(2,1)} %bitcast.248, bf16[128,2,64]{0,2,1:T(8,128)(2,1)} %bitcast.256, bf16[2048,2,64]{0,2,1:T(8,128)(2,1)} %bitcast.250, f32[2,128,2048]{2,1,0:T(8,128)S(1)} %get-tuple-element.111, f32[2,128]{1,0:T(2,128)S(1)} %bitcast.261, f32[2,128]{1,0:T(2,128)S(1)} %log_add_fusion), kind=kOutput, calls=%fused_computation.54 | convolution fusion | flops 136855552 | bytes 3213312 | tf_op jit(solution)/shard_map/while/body/eval_jaxpr/hqk,khd->qhd/dot_general | solution.py:110
  131.6 1.8 convolution_add_fusion.10
  133.4 17.6 %all_gather.21 = f32[2048,2]{0,1:T(2,128)S(1)} all-gather(f32[128,2]{0,1:T(2,128)S(1)} %fusion.101), channel_id=1, replica_groups=mesh['groups'=2,'tile'=16] {'tile'}, dimensions={0}, use_global_device_ids=true | all-gather | bytes 17408 | tf_op jit(solution)/shard_map/all_gather | solution.py:117
  151.0 2.0 fusion.3
  154.0 2.9 %fusion.15 = bf16[2,64,128]{2,1,0:T(8,128)(2,1)} fusion(bf16[2048,2,64]{0,2,1:T(8,128)(2,1)} %bitcast.244, f32[2,2048,128]{2,1,0:T(8,128)S(1)} %fusion.3, bf16[2048,2,64]{0,2,1:T(8,128)(2,1)} %bitcast.245, bf16[128,2,64]{0,2,1:T(8,128)(2,1)S(1)} %bitcast.251, f32[2,2048]{1,0:T(2,128)} %bitcast.258), kind=kOutput, calls=%fused_computation.55 | convolution fusion | flops 136331264 | bytes 3227648 | tf_op jit(solution)/shard_map/while/body/eval_jaxpr/hqk,qhd->khd/dot_general | solution.py:147
  156.9 1.2 convolution_add_fusion.9
  158.1 1.1 fusion.12
  159.2 1.0 convolution_bitcast_fusion
  160.2 1.0 convolution_bitcast_fusion.1
  161.3 1.0 convolution_bitcast_fusion.2
  162.3 1.0 convolution_bitcast_fusion.6
  168.2 1.6 pad_maximum_fusion
  170.7 7.4 %scatter_fusion = f32[3,257,256]{2,1,0:T(8,128)S(1)} fusion(f32[3,257,256]{2,1,0:T(8,128)S(1)} %broadcast_in_dim.38, s32[128]{0:T(128)S(1)} %get-tuple-element.116, f32[128,256]{1,0:T(8,128)S(1)} %copy-done.20), kind=kCustom, calls=%fused_computation | custom fusion | flops 32768 | bytes 394240 | tf_op jit(solution)/shard_map/scatter-add | solution.py:167
  178.2 7.4 %scatter_fusion.1 = f32[3,257,256]{2,1,0:T(8,128)S(1)} fusion(f32[3,257,256]{2,1,0:T(8,128)S(1)} %scatter_fusion, s32[128]{0:T(128)S(1)} %get-tuple-element.128, f32[128,256]{1,0:T(8,128)S(1)} %copy-done.19), kind=kCustom, calls=%fused_computation.1 | custom fusion | flops 32768 | bytes 394240 | tf_op jit(solution)/shard_map/scatter-add | solution.py:167
  185.6 7.4 %scatter_fusion.2 = f32[3,257,256]{2,1,0:T(8,128)S(1)} fusion(f32[3,257,256]{2,1,0:T(8,128)S(1)} %scatter_fusion.1, s32[128]{0:T(128)S(1)} %get-tuple-element.130, f32[128,256]{1,0:T(8,128)S(1)} %copy-done.18), kind=kCustom, calls=%fused_computation.2 | custom fusion | flops 32768 | bytes 394240 | tf_op jit(solution)/shard_map/scatter-add | solution.py:167
  193.1 7.4 %scatter_fusion.3 = f32[3,257,256]{2,1,0:T(8,128)S(1)} fusion(f32[3,257,256]{2,1,0:T(8,128)S(1)} %scatter_fusion.2, s32[128]{0:T(128)S(1)} %get-tuple-element.117, f32[128,256]{1,0:T(8,128)S(1)} %copy-done.17), kind=kCustom, calls=%fused_computation.3 | custom fusion | flops 32768 | bytes 394240 | tf_op jit(solution)/shard_map/scatter-add | solution.py:167
  200.5 7.4 %scatter_fusion.4 = f32[3,257,256]{2,1,0:T(8,128)S(1)} fusion(f32[3,257,256]{2,1,0:T(8,128)S(1)} %scatter_fusion.3, s32[128]{0:T(128)S(1)} %get-tuple-element.129, f32[128,256]{1,0:T(8,128)S(1)} %fusion.40), kind=kCustom, calls=%fused_computation.4 | custom fusion | flops 32768 | bytes 394240 | tf_op jit(solution)/shard_map/scatter-add | solution.py:167
  208.0 7.4 %scatter_fusion.5 = f32[3,257,256]{2,1,0:T(8,128)S(1)} fusion(f32[3,257,256]{2,1,0:T(8,128)S(1)} %scatter_fusion.4, s32[128]{0:T(128)S(1)} %get-tuple-element.131, f32[128,256]{1,0:T(8,128)S(1)} %fusion.37), kind=kCustom, calls=%fused_computation.5 | custom fusion | flops 32768 | bytes 394240 | tf_op jit(solution)/shard_map/scatter-add | solution.py:167
  215.6 7.5 %scatter_fusion.6 = f32[3,257,256]{2,1,0:T(8,128)S(1)} fusion(f32[3,257,256]{2,1,0:T(8,128)S(1)} %scatter_fusion.5, s32[128]{0:T(128)S(1)} %fusion.119, f32[128,256]{1,0:T(8,128)S(1)} %fusion.34), kind=kCustom, calls=%fused_computation.6 | custom fusion | flops 32768 | bytes 394240 | tf_op jit(solution)/shard_map/scatter-add | solution.py:167
  223.3 7.5 %scatter_fusion.7 = f32[3,257,256]{2,1,0:T(8,128)S(1)} fusion(f32[3,257,256]{2,1,0:T(8,128)S(1)} %scatter_fusion.6, s32[128]{0:T(128)S(1)} %fusion.120, f32[128,256]{1,0:T(8,128)S(1)} %fusion.31), kind=kCustom, calls=%fused_computation.7 | custom fusion | flops 32768 | bytes 394240 | tf_op jit(solution)/shard_map/scatter-add | solution.py:167
  230.9 7.4 %scatter_fusion.8 = f32[3,257,256]{2,1,0:T(8,128)S(1)} fusion(f32[3,257,256]{2,1,0:T(8,128)S(1)} %scatter_fusion.7, s32[128]{0:T(128)S(1)} %fusion.121, f32[128,256]{1,0:T(8,128)S(1)} %fusion.28), kind=kCustom, calls=%fused_computation.8 | custom fusion | flops 32768 | bytes 394240 | tf_op jit(solution)/shard_map/scatter-add | solution.py:167
  238.5 1.3 collective-permute-start.1
  240.6 1.1 collective-permute-done.1
  241.8 26.2 %all-reduce.12.cloned.1.call-done = f32[3,3,256,256]{3,2,1,0:T(8,128)} async-done(((f32[3,3,256,256]{3,2,1,0:T(8,128)}), f32[3,3,256,256]{3,2,1,0:T(8,128)}) %all-reduce.12.cloned.1.call-update) | async-done | bytes 2359312 | tf_op jit(solution)/shard_map/psum | solution.py:172
  267.9 3.3 %broadcast_multiply_fusion = f32[3,3,256,256]{3,2,1,0:T(8,128)} fusion(f32[3,3,256,256]{3,2,1,0:T(8,128)} %all-reduce.12.cloned.1.call-done), kind=kLoop, calls=%fused_computation.27 | loop fusion | flops 589824 | bytes 4718592 | tf_op jit(solution)/shard_map/mul | solution.py:172
  (123 shorter events, 17.2 us)
Async XLA Ops:
  7.2 80.3 %copy-start = (bf16[128,256]{1,0:T(8,128)(2,1)S(1)}, bf16[128,256]{1,0:T(8,128)(2,1)}, u32[]{:S(2)}) copy-start(bf16[128,256]{1,0:T(8,128)(2,1)} %param.12) | copy-start | bytes 196612
  7.2 6.7 %copy-start.1 = (bf16[3,3,256,256]{3,2,1,0:T(8,128)(2,1)S(1)}, bf16[3,3,256,256]{3,2,1,0:T(8,128)(2,1)}, u32[]{:S(2)}) copy-start(bf16[3,3,256,256]{3,2,1,0:T(8,128)(2,1)} %param.9) | copy-start | bytes 3538948
  7.2 260.8 %all-reduce.12.cloned.1.call-start = ((), (), s32[]{:S(2)}) async-start(), calls=%async_computation | async-start | bytes 4718592 | tf_op jit(solution)/shard_map/psum | solution.py:172
  8.2 3.3 %collective-permute-start = (bf16[1,256,256]{2,1,0:T(8,128)(2,1)S(1)}, bf16[1,256,256]{2,1,0:T(8,128)(2,1)S(1)}, u32[]{:S(2)}, u32[]{:S(2)}) collective-permute-start(bf16[1,256,256]{2,1,0:T(8,128)(2,1)S(1)} %slice.115), channel_id=1, source_target_pairs={{0,1},{1,2},{2,3},{3,4},{4,5},{5,6},{6,7},{7,8},{8,9},{9,10},{10,1... | collective-permute-start | bytes 393224 | tf_op jit(solution)/shard_map/ppermute | solution.py:16
  12.8 2.5 copy-start.5
  12.9 2.4 copy-start.9
  13.0 2.2 copy-start.13
  13.3 2.2 copy-start.7
  13.5 2.0 copy-start.11
  13.6 1.9 copy-start.14
  13.6 1.9 copy-start.21
  13.7 2.0 copy-start.15
  13.9 2.1 copy-start.16
  16.0 47.7 %copy-start.24 = (bf16[128,128]{0,1:T(8,128)(2,1)}, bf16[128,128]{0,1:T(8,128)(2,1)S(1)}, u32[]{:S(2)}) copy-start(bf16[128,128]{0,1:T(8,128)(2,1)S(1)} %convolution_convert_fusion.3) | copy-start | bytes 98308
  43.4 20.3 %copy-start.3 = (bf16[2048,128]{0,1:T(8,128)(2,1)}, bf16[2048,128]{0,1:T(8,128)(2,1)S(1)}, u32[]{:S(2)}) copy-start(bf16[2048,128]{0,1:T(8,128)(2,1)S(1)} %all_gather.19) | copy-start | bytes 1572868
  63.7 1.0 copy-start.27
  64.7 22.8 %copy-start.26 = (bf16[128,256]{1,0:T(8,128)(2,1)S(1)}, bf16[128,256]{1,0:T(8,128)(2,1)}, u32[]{:S(2)}) copy-start(bf16[128,256]{1,0:T(8,128)(2,1)} %param.13) | copy-start | bytes 196612
  85.5 0.8 copy-start.4
  86.9 0.6 copy-start.22
  87.7 0.6 copy-start.28
  131.6 21.4 %copy-start.2 = (bf16[2048,128]{0,1:T(8,128)(2,1)S(1)}, bf16[2048,128]{0,1:T(8,128)(2,1)}, u32[]{:S(2)}) copy-start(bf16[2048,128]{0,1:T(8,128)(2,1)} %all_gather.22) | copy-start | bytes 1572868
  156.9 6.5 %copy-start.10 = (bf16[1,128,256]{2,1,0:T(8,128)(2,1)S(1)}, bf16[1,128,256]{2,1,0:T(8,128)(2,1)}, u32[]{:S(2)}) copy-start(bf16[1,128,256]{2,1,0:T(8,128)(2,1)} %copy-done.9) | copy-start | bytes 196612
  156.9 6.7 %copy-start.6 = (bf16[1,128,256]{2,1,0:T(8,128)(2,1)S(1)}, bf16[1,128,256]{2,1,0:T(8,128)(2,1)}, u32[]{:S(2)}) copy-start(bf16[1,128,256]{2,1,0:T(8,128)(2,1)} %copy-done.5) | copy-start | bytes 196612
  156.9 6.9 %copy-start.12 = (bf16[1,128,256]{2,1,0:T(8,128)(2,1)S(1)}, bf16[1,128,256]{2,1,0:T(8,128)(2,1)}, u32[]{:S(2)}) copy-start(bf16[1,128,256]{2,1,0:T(8,128)(2,1)} %copy-done.11) | copy-start | bytes 196612
  156.9 7.1 %copy-start.8 = (bf16[1,128,256]{2,1,0:T(8,128)(2,1)S(1)}, bf16[1,128,256]{2,1,0:T(8,128)(2,1)}, u32[]{:S(2)}) copy-start(bf16[1,128,256]{2,1,0:T(8,128)(2,1)} %copy-done.7) | copy-start | bytes 196612
  169.8 0.9 copy-start.20
  169.8 8.3 %copy-start.19 = (f32[128,256]{1,0:T(8,128)S(1)}, f32[128,256]{1,0:T(8,128)}, u32[]{:S(2)}) copy-start(f32[128,256]{1,0:T(8,128)} %fusion.49) | copy-start | bytes 393220
  170.7 14.9 %copy-start.18 = (f32[128,256]{1,0:T(8,128)S(1)}, f32[128,256]{1,0:T(8,128)}, u32[]{:S(2)}) copy-start(f32[128,256]{1,0:T(8,128)} %fusion.46) | copy-start | bytes 393220
  178.2 14.9 %copy-start.17 = (f32[128,256]{1,0:T(8,128)S(1)}, f32[128,256]{1,0:T(8,128)}, u32[]{:S(2)}) copy-start(f32[128,256]{1,0:T(8,128)} %fusion.43) | copy-start | bytes 393220
  230.7 9.0 %copy-start.23 = (bf16[2,64,128]{2,1,0:T(8,128)(2,1)S(1)}, bf16[2,64,128]{2,1,0:T(8,128)(2,1)}, u32[]{:S(2)}) copy-start(bf16[2,64,128]{2,1,0:T(8,128)(2,1)} %copy-done.22) | copy-start | bytes 98308
  238.5 3.2 %collective-permute-start.1 = (bf16[1,256,256]{2,1,0:T(8,128)(2,1)S(1)}, bf16[1,256,256]{2,1,0:T(8,128)(2,1)S(1)}, u32[]{:S(2)}, u32[]{:S(2)}) collective-permute-start(bf16[1,256,256]{2,1,0:T(8,128)(2,1)S(1)} %slice.306), channel_id=1, source_target_pairs={{1,0},{2,1},{3,2},{4,3},{5,4},{6,5},{7,6},{8,7},{9,8},{10,9},{11,1... | collective-permute-start | bytes 393224 | tf_op jit(solution)/shard_map/ppermute | solution.py:16
  241.8 29.5 %copy-start.25 = (bf16[2,256,256]{2,1,0:T(8,128)(2,1)}, bf16[2,256,256]{2,1,0:T(8,128)(2,1)S(1)}, u32[]{:S(2)}) copy-start(bf16[2,256,256]{2,1,0:T(8,128)(2,1)S(1)} %fusion.27) | copy-start | bytes 786436
Sparse Core Ops, SparseCore 0:
  170.0 97.9 all-reduce.11
where the time goes:
time: 279 us; the launch traced here: 278 us
  blocking collectives  126 us (45%)
  other arithmetic  73.6 us (26%)
  waiting for transfers between devices  28.1 us (10%)
  matrix products  26.5 us (9%)
  between operations  14.8 us (5%)
  local copies, waits for them, and re-layouts  5.04 us (2%)
  starting transfers between devices  3.69 us (1%)
    scatter-add x9, other arithmetic, body(): dpadded.at[a:a + 2 * rows:2, b:b + 2 * cols:2]  66.9 us
    all_gather x1, blocking collectives, body(): lax.all_gather(key_loc, 'tile', axis=0, tiled=True)  27.5 us
    psum x1, waiting for transfers between devices, body(): grad_conv = lax.psum(kernel_local, 'tile') * (1.0 / math.sqrt(everyone))  26.2 us
    all_gather x1, blocking collectives, body(): lax.all_gather(value_loc, 'tile', axis=0, tiled=True)  20.5 us
    all_gather x1, blocking collectives, body(): lax.all_gather(delta.T, 'tile', axis=0, tiled=True)  20.3 us
    all_gather x1, blocking collectives, body(): d_in = lax.all_gather(dattended, 'tile', axis=0, tiled=True)  20.3 us
    all_gather x1, blocking collectives, body(): q_in = lax.all_gather(query, 'tile', axis=0, tiled=True)  20.3 us
    all_gather x1, blocking collectives, body(): lax.all_gather(lse.T, 'tile', axis=0, tiled=True)  17.6 us
  transfers between devices with their start and end apart: 3, of which 3 were waited for; matrix products, arithmetic and copies ran while one was open for 25% of the time, Pallas kernels for 0%

commit v1 on v0

--- a/solution.py
+++ b/solution.py
@@ -1,8 +1,11 @@
+import functools
 import math
 
 import jax
 import jax.numpy as jnp
 from jax import lax
+from jax.experimental import pallas as pl
+from jax.experimental.pallas import tpu as pltpu
 from jax.sharding import PartitionSpec as P
 
 HEADS = 2
@@ -176,22 +179,370 @@
     return (block_out, grad_conv, grad_fine.astype(jnp.bfloat16))
 
 
+NT = (((1,), (1,)), ((), ()))
+NN = (((1,), (0,)), ((), ()))
+
+
+def mm(left, right, dims=NN):
+    return lax.dot_general(left, right, dims, preferred_element_type=jnp.float32)
+
+
+def two_heads(mat):
+    lane = lax.broadcasted_iota(jnp.int32, mat.shape, 1)
+    zero = jnp.zeros_like(mat)
+    return jnp.concatenate(
+        [jnp.where(lane < HDIM, mat, zero), jnp.where(lane < HDIM, zero, mat)], axis=0
+    )
+
+
+def pick_heads(mat):
+    half = mat.shape[0] // 2
+    lane = lax.broadcasted_iota(jnp.int32, (half, mat.shape[1]), 1)
+    return jnp.where(lane < HDIM, mat[:half], mat[half:])
+
+
+class Gather:
+    def __init__(self, view, me, peers, send, recv, slot):
+        self.view, self.peers, self.send, self.recv, self.slot = view, peers, send, recv, slot
+        self.zs = peers // 4
+        self.core = lax.rem(me, 2)
+        self.x = lax.rem(lax.div(me, 2), 2)
+        self.z = lax.div(me, 4)
+        self.me = me
+        self.copies = []
+
+    def at(self, dz, flip_x=0, flip_core=0):
+        z = lax.rem(self.z + dz + self.zs, self.zs)
+        x = 1 - self.x if flip_x else self.x
+        core = 1 - self.core if flip_core else self.core
+        return z * 4 + x * 2 + core
+
+    def copy(self, index, block, target):
+        return pltpu.make_async_remote_copy(
+            src_ref=self.view(block),
+            dst_ref=self.view(block),
+            send_sem=self.send.at[self.slot, index],
+            recv_sem=self.recv.at[self.slot, index],
+            device_id={"tile": target},
+            device_id_type=pl.DeviceIdType.MESH,
+        )
+
+    def go(self, index, block, target):
+        made = self.copy(index, block, target)
+        made.start()
+        self.copies.append(made)
+
+    def landed(self, index, block):
+        self.copy(index, block, self.at(0, 1)).wait_recv()
+
+    def own(self):
+        zs = self.zs
+        for d in range(1, zs):
+            self.go(d - 1, self.me, self.at(d))
+        self.go(zs - 1, self.me, self.at(0, 1))
+        self.go(2 * zs - 1, self.me, self.at(0, 0, 1))
+
+    def across(self):
+        zs = self.zs
+        for d in range(1, zs):
+            block = self.at(-d)
+            self.landed(d - 1, block)
+            self.go(zs - 1 + d, block, self.at(0, 1))
+            self.go(2 * zs - 1 + d, block, self.at(0, 0, 1))
+
+    def over(self):
+        zs = self.zs
+        for d in range(zs):
+            block = self.at(-d, 1)
+            self.landed(zs - 1 + d, block)
+            self.go(3 * zs - 1 + d, block, self.at(0, 0, 1))
+
+    def finish(self):
+        zs = self.zs
+        for d in range(zs):
+            self.landed(2 * zs - 1 + d, self.at(-d, 0, 1))
+            self.landed(3 * zs - 1 + d, self.at(-d, 1, 1))
+
+    def drain(self):
+        for made in self.copies:
+            made.wait_send()
+
+
+def fused_kernel(
+    peers,
+    fine,
+    conv,
+    qk,
+    vw,
+    ow,
+    up,
+    block_out,
+    grad_conv,
+    grad_fine,
+    above,
+    kv_all,
+    qd_all,
+    dh_all,
+    shift_all,
+    fine_t,
+    stats,
+    st_buf,
+    dpt_buf,
+    send,
+    recv,
+    stat_send,
+    stat_recv,
+    halo_send,
+    halo_recv,
+):
+    me = lax.axis_index("tile")
+    n = up.shape[0]
+    chans = up.shape[1]
+    full = n * peers
+    lower = lax.rem(me + 1, peers)
+    upper = lax.rem(me + peers - 1, peers)
+
+    barrier = pltpu.get_barrier_semaphore()
+    for step in range(1, peers):
+        pl.semaphore_signal(
+            barrier,
+            inc=1,
+            device_id={"tile": lax.rem(me + step, peers)},
+            device_id_type=pl.DeviceIdType.MESH,
+        )
+
+    def rows(ref):
+        return lambda t: ref.at[pl.ds(pl.multiple_of(t * n, n), n), :]
+
+    def cols(ref):
+        return lambda t: ref.at[:, pl.ds(pl.multiple_of(t * n, n), n)]
+
+    mine = pl.ds(pl.multiple_of(me * n, n), n)
+    for r in range(2):
+        fine_t[r * 2 * chans : (r + 1) * 2 * chans, mine] = fine[r].T
+    pl.semaphore_wait(barrier, peers - 1)
+    halo = pltpu.make_async_remote_copy(
+        src_ref=fine.at[1],
+        dst_ref=above,
+        send_sem=halo_send,
+        recv_sem=halo_recv,
+        device_id={"tile": lower},
+        device_id_type=pl.DeviceIdType.MESH,
+    )
+    halo.start()
+    fine_gather = Gather(cols(fine_t), me, peers, send, recv, 0)
+    kv_gather = Gather(rows(kv_all), me, peers, send, recv, 1)
+    qd_gather = Gather(rows(qd_all), me, peers, send, recv, 2)
+    dh_gather = Gather(rows(dh_all), me, peers, send, recv, 3)
+
+    def conv_row(a, row):
+        straight = mm(row[:, :chans], conv[a, 1]) + mm(row[:, chans:], conv[a, 2])
+        return straight, mm(row[:, chans:], conv[a, 0])
+
+    mid, mid_late = conv_row(1, fine[0])
+    low, low_late = conv_row(2, fine[1])
+    dattended = mm(up[...], ow[...], NT).astype(jnp.bfloat16)
+    halo.wait_recv()
+    top_row = jnp.where(me == 0, jnp.zeros_like(above[...]), above[...])
+    top, top_late = conv_row(0, top_row)
+    late = top_late + mid_late + low_late
+    row_at = lax.broadcasted_iota(jnp.int32, (n, chans), 0)
+    late = jnp.where(row_at == 0, 0.0, pltpu.roll(late, 1, 0))
+    hidden = (top + mid + low + late).astype(jnp.bfloat16)
+    keys = mm(hidden, qk[1]).astype(jnp.bfloat16)
+    values = mm(hidden, vw[...]).astype(jnp.bfloat16)
+    kv_all[mine, :] = jnp.concatenate([keys, values], axis=1)
+    kv_gather.own()
+    query = (mm(hidden, qk[0]).astype(jnp.bfloat16) * jnp.bfloat16(HDIM**-0.5)).astype(jnp.bfloat16)
+    qd_all[mine, :] = jnp.concatenate([query, dattended], axis=1)
+    kv_gather.across()
+    kv_gather.over()
+    qd_gather.own()
+    kv_gather.finish()
+    fine_gather.own()
+
+    q2 = two_heads(query)
+    d2 = two_heads(dattended)
+    scores = mm(q2, kv_all[:, :HD], NT)
+    high = jnp.max(scores, axis=1, keepdims=True)
+    expd = jnp.exp(scores - high)
+    total = jnp.sum(expd, axis=1, keepdims=True)
+    lse = high + jnp.log(total)
+    prob = expd * (1.0 / total)
+    attended = pick_heads(mm(prob.astype(jnp.bfloat16), kv_all[:, HD:])).astype(jnp.bfloat16)
+    product = dattended.astype(jnp.float32) * attended.astype(jnp.float32)
+    delta = jnp.sum(two_heads(product), axis=1, keepdims=True)
+    lane = lax.broadcasted_iota(jnp.int32, (2 * n, 128), 1)
+    packed = jnp.where(lane == 0, lse, jnp.where(lane == 1, delta, 0.0)).T
+    stats[me] = packed[:2]
+    stat_copies = []
+    for step in range(1, peers):
+        made = pltpu.make_async_remote_copy(
+            src_ref=stats.at[me],
+            dst_ref=stats.at[me],
+            send_sem=stat_send.at[step],
+            recv_sem=stat_recv.at[step],
+            device_id={"tile": lax.rem(me + step, peers)},
+            device_id_type=pl.DeviceIdType.MESH,
+        )
+        made.start()
+        stat_copies.append(made)
+    qd_gather.across()
+    qd_gather.over()
+    block_out[...] = (hidden.astype(jnp.float32) + mm(attended, ow[...])).astype(jnp.bfloat16)
+    dprob = mm(d2, kv_all[:, HD:], NT)
+    dscore = (prob * (dprob - delta)).astype(jnp.bfloat16)
+    dquery = (pick_heads(mm(dscore, kv_all[:, :HD])) * HDIM**-0.5).astype(jnp.bfloat16)
+    grad_h = up[...].astype(jnp.float32) + mm(dquery, qk[0], NT)
+    qd_gather.finish()
+    fine_gather.across()
+
+    k2 = two_heads(keys)
+    v2 = two_heads(values)
+    st_buf[...] = mm(k2, qd_all[:, :HD], NT)
+    dpt_buf[...] = mm(v2, qd_all[:, HD:], NT)
+    for step in range(1, peers):
+        block = lax.rem(me - step + peers, peers)
+        pltpu.make_async_remote_copy(
+            src_ref=stats.at[block],
+            dst_ref=stats.at[block],
+            send_sem=stat_send.at[step],
+            recv_sem=stat_recv.at[step],
+            device_id={"tile": lower},
+            device_id_type=pl.DeviceIdType.MESH,
+        ).wait_recv()
+    dk = jnp.zeros((2 * n, HD), jnp.float32)
+    dv = jnp.zeros((2 * n, HD), jnp.float32)
+    group = math.gcd(peers, 4)
+    for at in range(0, peers, group):
+        span = slice(at * n, (at + group) * n)
+
+        def stat_rows(kind):
+            heads = []
+            for h in range(HEADS):
+                parts = [stats[t, kind : kind + 1, h * n : (h + 1) * n] for t in range(at, at + group)]
+                heads.append(jnp.broadcast_to(jnp.concatenate(parts, axis=1), (n, group * n)))
+            return jnp.concatenate(heads, axis=0)
+
+        prob_t = jnp.exp(st_buf[:, span] - stat_rows(0))
+        dscore_t = (prob_t * (dpt_buf[:, span] - stat_rows(1))).astype(jnp.bfloat16)
+        dv = dv + mm(prob_t.astype(jnp.bfloat16), qd_all[span, HD:])
+        dk = dk + mm(dscore_t, qd_all[span, :HD])
+    dkeys = pick_heads(dk).astype(jnp.bfloat16)
+    dvalues = pick_heads(dv).astype(jnp.bfloat16)
+    grad_h = grad_h + mm(dkeys, qk[1], NT) + mm(dvalues, vw[...], NT)
+    dhidden = grad_h.astype(jnp.bfloat16)
+    dh_all[mine, :] = dhidden
+    dh_gather.own()
+
+    def back_row(a, grads):
+        even = mm(grads, conv[a, 1], NT)
+        later = mm(grads, conv[a, 0], NT)
+        later = jnp.where(row_at == n - 1, 0.0, pltpu.roll(later, n - 1, 0))
+        return even, mm(grads, conv[a, 2], NT) + later
+
+    even_mid, odd_mid = back_row(1, dhidden)
+    grad_fine[0, :, :chans] = even_mid.astype(jnp.bfloat16)
+    grad_fine[0, :, chans:] = odd_mid.astype(jnp.bfloat16)
+    even_low, odd_low = back_row(2, dhidden)
+    dh_gather.across()
+    fine_gather.over()
+    dh_gather.over()
+    dh_gather.finish()
+    below = dh_all[pl.ds(pl.multiple_of(lower * n, n), n), :]
+    below = jnp.where(me == peers - 1, jnp.zeros_like(below), below)
+    even_top, odd_top = back_row(0, below)
+    grad_fine[1, :, :chans] = (even_low + even_top).astype(jnp.bfloat16)
+    grad_fine[1, :, chans:] = (odd_low + odd_top).astype(jnp.bfloat16)
+    for t in range(peers):
+        span = slice(t * n, (t + 1) * n)
+        moved = pltpu.roll(dh_all[span, :].astype(jnp.float32), n - 1, 0)
+        shift_all[span, :] = jnp.where(row_at == n - 1, 0.0, moved).astype(jnp.bfloat16)
+    fine_gather.finish()
+    norm = 1.0 / math.sqrt(full)
+    for a, row in ((1, 0), (2, 1), (0, 1)):
+        for b in range(3):
+            source = dh_all if b else shift_all
+            at = row * 2 * chans + (0 if b == 1 else chans)
+            features = slice(at, at + chans)
+            if a == 0:
+                part = mm(fine_t[features, : full - n], source[n:, :])
+            else:
+                part = mm(fine_t[features, :], source[...])
+            grad_conv[3 * a + b] = part * norm
+    halo.wait_send()
+    for gather in (fine_gather, kv_gather, qd_gather, dh_gather):
+        gather.drain()
+    for made in stat_copies:
+        made.wait_send()
+
+
+def fused_body(fine, conv_weight, qk_weight, v_weight, o_weight, upstream):
+    peers = lax.axis_size("tile")
+    n, chans = upstream.shape
+    full = n * peers
+    pairs = fine.reshape(2, n, 2 * chans)
+    vmem = pl.BlockSpec(memory_space=pltpu.VMEM)
+    dma = pltpu.SemaphoreType.DMA
+    block_out, grad_conv, grad_fine = pl.pallas_call(
+        functools.partial(fused_kernel, peers),
+        out_shape=(
+            jax.ShapeDtypeStruct((n, chans), jnp.bfloat16),
+            jax.ShapeDtypeStruct((9, chans, chans), jnp.float32),
+            jax.ShapeDtypeStruct((2, n, 2 * chans), jnp.bfloat16),
+        ),
+        in_specs=[vmem] * 6,
+        out_specs=(vmem, vmem, vmem),
+        scratch_shapes=[
+            pltpu.VMEM((n, 2 * chans), jnp.bfloat16),
+            pltpu.VMEM((full, 2 * HD), jnp.bfloat16),
+            pltpu.VMEM((full, 2 * HD), jnp.bfloat16),
+            pltpu.VMEM((full, chans), jnp.bfloat16),
+            pltpu.VMEM((full, chans), jnp.bfloat16),
+            pltpu.VMEM((4 * chans, full), jnp.bfloat16),
+            pltpu.VMEM((peers, 2, 2 * n), jnp.float32),
+            pltpu.VMEM((2 * n, full), jnp.float32),
+            pltpu.VMEM((2 * n, full), jnp.float32),
+            dma((4, peers)),
+            dma((4, peers)),
+            dma((peers,)),
+            dma((peers,)),
+            dma,
+            dma,
+        ],
+        compiler_params=pltpu.CompilerParams(
+            collective_id=0, has_side_effects=True, vmem_limit_bytes=48 * 2**20
+        ),
+    )(pairs, conv_weight, qk_weight, v_weight, o_weight, upstream)
+    return (
+        block_out,
+        grad_conv.reshape(3, 3, chans, chans),
+        grad_fine.reshape(fine.shape),
+    )
+
+
 def solution(mesh):
-    return jax.shard_map(
-        body,
-        mesh=mesh,
-        in_specs=(
-            P(("groups", "tile"), None, None),
-            P(),
-            P(),
-            P(),
-            P(),
-            P(("groups", "tile"), None),
-        ),
-        out_specs=(
-            P(("groups", "tile"), None),
-            P("groups", None, None, None),
-            P(("groups", "tile"), None, None),
-        ),
-        check_vma=False,
-    )
+    def whole(fine, *rest):
+        devices = mesh.shape["groups"] * mesh.shape["tile"]
+        one_row = fine.shape[0] == 2 * devices and fine.shape[1] == 256 and fine.shape[2] == 256
+        fits = fine.size // mesh.shape["groups"] <= 4 * 2**20 and mesh.shape["tile"] % 4 == 0
+        return jax.shard_map(
+            fused_body if one_row and fits else body,
+            mesh=mesh,
+            in_specs=(
+                P(("groups", "tile"), None, None),
+                P(),
+                P(),
+                P(),
+                P(),
+                P(("groups", "tile"), None),
+            ),
+            out_specs=(
+                P(("groups", "tile"), None),
+                P("groups", None, None, None),
+                P(("groups", "tile"), None, None),
+            ),
+            check_vma=False,
+        )(fine, *rest)
+
+    return whole

time: 279 us -> 78 us (0.28)
  the two profiles are of different devices: /device:TPU:0 before, /device:TPU:11 now
where the time goes in v1:
time: 78 us; the launch traced here: 77.7 us
  Pallas kernels  68.5 us (88%)
  local copies, waits for them, and re-layouts  8.55 us (11%)
    pallas_call x1, Pallas kernels, fused_body(): pl.pallas_call(functools.partial(fused_kernel, peers), out_shape=(jax.Sha...  68.5 us
    unnamed x12, local copies, waits for them, and re-layouts  6.72 us

profile of v1, /device:TPU:11, one launch (start us, length us, event | category | flops | bytes accessed | tf_op | source)
XLA Modules:
  0.0 77.7 jit_solution(6620960719921939961)
XLA Ops:
  0.6 1.0 %reshape.15.fine = bf16[2,128,512]{2,1,0:T(8,128)(2,1)S(1)} reshape(bf16[2,256,256]{2,1,0:T(8,128)(2,1)} %param.6) | data formatting | bytes 524288 | tf_op jit(solution)/shard_map/reshape | solution.py:484
  1.7 0.0 copy-start
  1.7 1.3 %copy-done = bf16[3,3,256,256]{3,2,1,0:T(8,128)(2,1)S(1)} copy-done((bf16[3,3,256,256]{3,2,1,0:T(8,128)(2,1)S(1)}, bf16[3,3,256,256]{3,2,1,0:T(8,128)(2,1)}, u32[]{:S(2)}) %copy-start) | copy-done | bytes 1179672
  2.9 0.0 copy-start.1
  2.9 0.9 %copy-done.1 = bf16[2,256,128]{2,1,0:T(8,128)(2,1)S(1)} copy-done((bf16[2,256,128]{2,1,0:T(8,128)(2,1)S(1)}, bf16[2,256,128]{2,1,0:T(8,128)(2,1)}, u32[]{:S(2)}) %copy-start.1) | copy-done | bytes 131096
  3.9 0.0 copy-start.2
  3.9 0.8 %copy-done.2 = bf16[256,128]{1,0:T(8,128)(2,1)S(1)} copy-done((bf16[256,128]{1,0:T(8,128)(2,1)S(1)}, bf16[256,128]{1,0:T(8,128)(2,1)}, u32[]{:S(2)}) %copy-start.2) | copy-done | bytes 65560
  4.7 0.0 copy-start.3
  4.7 0.8 %copy-done.3 = bf16[128,256]{1,0:T(8,128)(2,1)S(1)} copy-done((bf16[128,256]{1,0:T(8,128)(2,1)S(1)}, bf16[128,256]{1,0:T(8,128)(2,1)}, u32[]{:S(2)}) %copy-start.3) | copy-done | bytes 65560
  5.5 0.0 copy-start.4
  5.5 0.8 %copy-done.4 = bf16[128,256]{1,0:T(8,128)(2,1)S(1)} copy-done((bf16[128,256]{1,0:T(8,128)(2,1)S(1)}, bf16[128,256]{1,0:T(8,128)(2,1)}, u32[]{:S(2)}) %copy-start.4) | copy-done | bytes 65560
  6.4 68.5 %shard_map.85 = (bf16[128,256]{1,0:T(8,128)(2,1)S(1)}, f32[9,256,256]{2,1,0:T(8,128)S(1)}, bf16[2,128,512]{2,1,0:T(8,128)(2,1)S(1)}) custom-call(bf16[2,128,512]{2,1,0:T(8,128)(2,1)S(1)} %reshape.15.fine, bf16[3,3,256,256]{3,2,1,0:T(8,128)(2,1)S(1)} %copy-done, bf16[2,256,128]{2,1,0:T(8,128)(2,1)S(1)} %copy-done.1, bf16[256,128]{1,0:T(8,128)(2,1)S(1)} %copy-done.2, ...), custom_call_target="tpu_custom_call" | custom-call | tf_op jit(solution)/shard_map/pallas_call | solution.py:487
  74.9 0.8 %reshape.17 = bf16[2,256,256]{2,1,0:T(8,128)(2,1)} reshape(bf16[2,128,512]{2,1,0:T(8,128)(2,1)S(1)} %get-tuple-element.8) | data formatting | bytes 524288 | tf_op jit(solution)/shard_map/reshape | solution.py:520
  75.6 0.6 copy.11
  76.3 1.4 %copy.12 = f32[3,3,256,256]{3,2,1,0:T(8,128)} copy(f32[3,3,256,256]{3,2,1,0:T(8,128)S(1)} %bitcast.1) | data formatting | bytes 4718592
Async XLA Ops:
  1.7 1.3 %copy-start = (bf16[3,3,256,256]{3,2,1,0:T(8,128)(2,1)S(1)}, bf16[3,3,256,256]{3,2,1,0:T(8,128)(2,1)}, u32[]{:S(2)}) copy-start(bf16[3,3,256,256]{3,2,1,0:T(8,128)(2,1)} %conv.1) | copy-start | bytes 3538948
  2.9 0.9 %copy-start.1 = (bf16[2,256,128]{2,1,0:T(8,128)(2,1)S(1)}, bf16[2,256,128]{2,1,0:T(8,128)(2,1)}, u32[]{:S(2)}) copy-start(bf16[2,256,128]{2,1,0:T(8,128)(2,1)} %qk.1) | copy-start | bytes 393220
  3.9 0.8 %copy-start.2 = (bf16[256,128]{1,0:T(8,128)(2,1)S(1)}, bf16[256,128]{1,0:T(8,128)(2,1)}, u32[]{:S(2)}) copy-start(bf16[256,128]{1,0:T(8,128)(2,1)} %vw.1) | copy-start | bytes 196612
  4.7 0.8 %copy-start.3 = (bf16[128,256]{1,0:T(8,128)(2,1)S(1)}, bf16[128,256]{1,0:T(8,128)(2,1)}, u32[]{:S(2)}) copy-start(bf16[128,256]{1,0:T(8,128)(2,1)} %ow.1) | copy-start | bytes 196612
  5.5 0.8 %copy-start.4 = (bf16[128,256]{1,0:T(8,128)(2,1)S(1)}, bf16[128,256]{1,0:T(8,128)(2,1)}, u32[]{:S(2)}) copy-start(bf16[128,256]{1,0:T(8,128)(2,1)} %up.1) | copy-start | bytes 196612

commit v2 on v1

--- a/solution.py
+++ b/solution.py
@@ -270,6 +270,15 @@
 
 def fused_kernel(
     peers,
+    fine_hbm,
+    conv_hbm,
+    qk_hbm,
+    vw_hbm,
+    ow_hbm,
+    up_hbm,
+    block_hbm,
+    grad_conv_hbm,
+    grad_fine_hbm,
     fine,
     conv,
     qk,
@@ -279,9 +288,13 @@
     block_out,
     grad_conv,
     grad_fine,
+    in_sem,
+    out_sem,
     above,
+    hid_all,
     kv_all,
-    qd_all,
+    q_all,
+    d_all,
     dh_all,
     shift_all,
     fine_t,
@@ -300,7 +313,18 @@
     chans = up.shape[1]
     full = n * peers
     lower = lax.rem(me + 1, peers)
-    upper = lax.rem(me + peers - 1, peers)
+    moves = (
+        (fine_hbm, fine), (up_hbm, up), (ow_hbm, ow), (conv_hbm, conv), (qk_hbm, qk), (vw_hbm, vw)
+    )
+    loads = [pltpu.make_async_copy(a, b, in_sem.at[i]) for i, (a, b) in enumerate(moves)]
+    for load in loads:
+        load.start()
+    stores = []
+
+    def store(source, target):
+        made = pltpu.make_async_copy(source, target, out_sem.at[len(stores)])
+        made.start()
+        stores.append(made)
 
     barrier = pltpu.get_barrier_semaphore()
     for step in range(1, peers):
@@ -314,12 +338,12 @@
     def rows(ref):
         return lambda t: ref.at[pl.ds(pl.multiple_of(t * n, n), n), :]
 
-    def cols(ref):
-        return lambda t: ref.at[:, pl.ds(pl.multiple_of(t * n, n), n)]
+    def cols(ref, part):
+        lines = pl.ds(part * chans, chans)
+        return lambda t: ref.at[lines, pl.ds(pl.multiple_of(t * n, n), n)]
 
     mine = pl.ds(pl.multiple_of(me * n, n), n)
-    for r in range(2):
-        fine_t[r * 2 * chans : (r + 1) * 2 * chans, mine] = fine[r].T
+    loads[0].wait()
     pl.semaphore_wait(barrier, peers - 1)
     halo = pltpu.make_async_remote_copy(
         src_ref=fine.at[1],
@@ -330,10 +354,14 @@
         device_id_type=pl.DeviceIdType.MESH,
     )
     halo.start()
-    fine_gather = Gather(cols(fine_t), me, peers, send, recv, 0)
-    kv_gather = Gather(rows(kv_all), me, peers, send, recv, 1)
-    qd_gather = Gather(rows(qd_all), me, peers, send, recv, 2)
-    dh_gather = Gather(rows(dh_all), me, peers, send, recv, 3)
+    fine_t[: 2 * chans, mine] = fine[0].T
+    parts = [Gather(cols(fine_t, p), me, peers, send, recv, i) for i, p in enumerate((0, 1, 3, 2))]
+    hid_gather = Gather(rows(hid_all), me, peers, send, recv, 4)
+    d_gather = Gather(rows(d_all), me, peers, send, recv, 5)
+    dh_gather = Gather(rows(dh_all), me, peers, send, recv, 6)
+    parts[0].own()
+    for load in loads[1:]:
+        load.wait()
 
     def conv_row(a, row):
         straight = mm(row[:, :chans], conv[a, 1]) + mm(row[:, chans:], conv[a, 2])
@@ -342,6 +370,7 @@
     mid, mid_late = conv_row(1, fine[0])
     low, low_late = conv_row(2, fine[1])
     dattended = mm(up[...], ow[...], NT).astype(jnp.bfloat16)
+    fine_t[2 * chans :, mine] = fine[1].T
     halo.wait_recv()
     top_row = jnp.where(me == 0, jnp.zeros_like(above[...]), above[...])
     top, top_late = conv_row(0, top_row)
@@ -349,20 +378,28 @@
     row_at = lax.broadcasted_iota(jnp.int32, (n, chans), 0)
     late = jnp.where(row_at == 0, 0.0, pltpu.roll(late, 1, 0))
     hidden = (top + mid + low + late).astype(jnp.bfloat16)
+    hid_all[mine, :] = hidden
+    hid_gather.own()
+    d_all[mine, :] = dattended
     keys = mm(hidden, qk[1]).astype(jnp.bfloat16)
     values = mm(hidden, vw[...]).astype(jnp.bfloat16)
-    kv_all[mine, :] = jnp.concatenate([keys, values], axis=1)
-    kv_gather.own()
-    query = (mm(hidden, qk[0]).astype(jnp.bfloat16) * jnp.bfloat16(HDIM**-0.5)).astype(jnp.bfloat16)
-    qd_all[mine, :] = jnp.concatenate([query, dattended], axis=1)
-    kv_gather.across()
-    kv_gather.over()
-    qd_gather.own()
-    kv_gather.finish()
-    fine_gather.own()
-
+
+    def scaled_query(mat):
+        full_query = mm(mat, qk[0]).astype(jnp.bfloat16)
+        return (full_query.astype(jnp.float32) * HDIM**-0.5).astype(jnp.bfloat16)
+
+    query = scaled_query(hidden)
     q2 = two_heads(query)
     d2 = two_heads(dattended)
+    parts[0].across()
+    hid_gather.across()
+    d_gather.own()
+    parts[1].own()
+    hid_gather.over()
+    parts[0].over()
+    hid_gather.finish()
+    kv_all[:, :HD] = mm(hid_all[...], qk[1]).astype(jnp.bfloat16)
+    kv_all[:, HD:] = mm(hid_all[...], vw[...]).astype(jnp.bfloat16)
     scores = mm(q2, kv_all[:, :HD], NT)
     high = jnp.max(scores, axis=1, keepdims=True)
     expd = jnp.exp(scores - high)
@@ -387,20 +424,23 @@
         )
         made.start()
         stat_copies.append(made)
-    qd_gather.across()
-    qd_gather.over()
+    d_gather.across()
     block_out[...] = (hidden.astype(jnp.float32) + mm(attended, ow[...])).astype(jnp.bfloat16)
+    store(block_out, block_hbm)
+    q_all[...] = scaled_query(hid_all[...])
+    d_gather.over()
+    parts[1].across()
+    parts[2].own()
     dprob = mm(d2, kv_all[:, HD:], NT)
     dscore = (prob * (dprob - delta)).astype(jnp.bfloat16)
     dquery = (pick_heads(mm(dscore, kv_all[:, :HD])) * HDIM**-0.5).astype(jnp.bfloat16)
     grad_h = up[...].astype(jnp.float32) + mm(dquery, qk[0], NT)
-    qd_gather.finish()
-    fine_gather.across()
+    d_gather.finish()
 
     k2 = two_heads(keys)
     v2 = two_heads(values)
-    st_buf[...] = mm(k2, qd_all[:, :HD], NT)
-    dpt_buf[...] = mm(v2, qd_all[:, HD:], NT)
+    st_buf[...] = mm(k2, q_all[...], NT)
+    dpt_buf[...] = mm(v2, d_all[...], NT)
     for step in range(1, peers):
         block = lax.rem(me - step + peers, peers)
         pltpu.make_async_remote_copy(
@@ -426,14 +466,17 @@
 
         prob_t = jnp.exp(st_buf[:, span] - stat_rows(0))
         dscore_t = (prob_t * (dpt_buf[:, span] - stat_rows(1))).astype(jnp.bfloat16)
-        dv = dv + mm(prob_t.astype(jnp.bfloat16), qd_all[span, HD:])
-        dk = dk + mm(dscore_t, qd_all[span, :HD])
+        dv = dv + mm(prob_t.astype(jnp.bfloat16), d_all[span, :])
+        dk = dk + mm(dscore_t, q_all[span, :])
     dkeys = pick_heads(dk).astype(jnp.bfloat16)
     dvalues = pick_heads(dv).astype(jnp.bfloat16)
     grad_h = grad_h + mm(dkeys, qk[1], NT) + mm(dvalues, vw[...], NT)
     dhidden = grad_h.astype(jnp.bfloat16)
     dh_all[mine, :] = dhidden
     dh_gather.own()
+    parts[1].over()
+    parts[2].across()
+    parts[3].own()
 
     def back_row(a, grads):
         even = mm(grads, conv[a, 1], NT)
@@ -446,8 +489,9 @@
     grad_fine[0, :, chans:] = odd_mid.astype(jnp.bfloat16)
     even_low, odd_low = back_row(2, dhidden)
     dh_gather.across()
-    fine_gather.over()
     dh_gather.over()
+    parts[2].over()
+    parts[3].across()
     dh_gather.finish()
     below = dh_all[pl.ds(pl.multiple_of(lower * n, n), n), :]
     below = jnp.where(me == peers - 1, jnp.zeros_like(below), below)
@@ -458,23 +502,40 @@
         span = slice(t * n, (t + 1) * n)
         moved = pltpu.roll(dh_all[span, :].astype(jnp.float32), n - 1, 0)
         shift_all[span, :] = jnp.where(row_at == n - 1, 0.0, moved).astype(jnp.bfloat16)
-    fine_gather.finish()
+    store(grad_fine, grad_fine_hbm)
     norm = 1.0 / math.sqrt(full)
-    for a, row in ((1, 0), (2, 1), (0, 1)):
-        for b in range(3):
-            source = dh_all if b else shift_all
-            at = row * 2 * chans + (0 if b == 1 else chans)
-            features = slice(at, at + chans)
-            if a == 0:
-                part = mm(fine_t[features, : full - n], source[n:, :])
-            else:
-                part = mm(fine_t[features, :], source[...])
-            grad_conv[3 * a + b] = part * norm
+
+    def finish_tap(a, b):
+        source = dh_all if b else shift_all
+        at = (2 if a != 1 else 0) * chans + (0 if b == 1 else chans)
+        features = slice(at, at + chans)
+        if a == 0:
+            part = mm(fine_t[features, : full - n], source[n:, :])
+        else:
+            part = mm(fine_t[features, :], source[...])
+        grad_conv[3 * a + b] = part * norm
+        store(grad_conv.at[3 * a + b], grad_conv_hbm.at[3 * a + b])
+
+    parts[0].finish()
+    finish_tap(1, 1)
+    parts[1].finish()
+    finish_tap(1, 2)
+    parts[3].over()
+    finish_tap(1, 0)
+    parts[2].finish()
+    for a in (2, 0):
+        for b in (2, 0):
+            finish_tap(a, b)
+    parts[3].finish()
+    for a in (2, 0):
+        finish_tap(a, 1)
     halo.wait_send()
-    for gather in (fine_gather, kv_gather, qd_gather, dh_gather):
+    for gather in (*parts, hid_gather, d_gather, dh_gather):
         gather.drain()
     for made in stat_copies:
         made.wait_send()
+    for made in stores:
+        made.wait()
 
 
 def fused_body(fine, conv_weight, qk_weight, v_weight, o_weight, upstream):
@@ -482,7 +543,7 @@
     n, chans = upstream.shape
     full = n * peers
     pairs = fine.reshape(2, n, 2 * chans)
-    vmem = pl.BlockSpec(memory_space=pltpu.VMEM)
+    hbm = pl.BlockSpec(memory_space=pl.ANY)
     dma = pltpu.SemaphoreType.DMA
     block_out, grad_conv, grad_fine = pl.pallas_call(
         functools.partial(fused_kernel, peers),
@@ -491,27 +552,40 @@
             jax.ShapeDtypeStruct((9, chans, chans), jnp.float32),
             jax.ShapeDtypeStruct((2, n, 2 * chans), jnp.bfloat16),
         ),
-        in_specs=[vmem] * 6,
-        out_specs=(vmem, vmem, vmem),
+        in_specs=[hbm] * 6,
+        out_specs=(hbm, hbm, hbm),
         scratch_shapes=[
+            pltpu.VMEM(pairs.shape, jnp.bfloat16),
+            pltpu.VMEM(conv_weight.shape, jnp.bfloat16),
+            pltpu.VMEM(qk_weight.shape, jnp.bfloat16),
+            pltpu.VMEM(v_weight.shape, jnp.bfloat16),
+            pltpu.VMEM(o_weight.shape, jnp.bfloat16),
+            pltpu.VMEM(upstream.shape, jnp.bfloat16),
+            pltpu.VMEM((n, chans), jnp.bfloat16),
+            pltpu.VMEM((9, chans, chans), jnp.float32),
+            pltpu.VMEM((2, n, 2 * chans), jnp.bfloat16),
+            dma((6,)),
+            dma((11,)),
             pltpu.VMEM((n, 2 * chans), jnp.bfloat16),
+            pltpu.VMEM((full, chans), jnp.bfloat16),
             pltpu.VMEM((full, 2 * HD), jnp.bfloat16),
-            pltpu.VMEM((full, 2 * HD), jnp.bfloat16),
+            pltpu.VMEM((full, HD), jnp.bfloat16),
+            pltpu.VMEM((full, HD), jnp.bfloat16),
             pltpu.VMEM((full, chans), jnp.bfloat16),
             pltpu.VMEM((full, chans), jnp.bfloat16),
             pltpu.VMEM((4 * chans, full), jnp.bfloat16),
             pltpu.VMEM((peers, 2, 2 * n), jnp.float32),
             pltpu.VMEM((2 * n, full), jnp.float32),
             pltpu.VMEM((2 * n, full), jnp.float32),
-            dma((4, peers)),
-            dma((4, peers)),
+            dma((7, peers)),
+            dma((7, peers)),
             dma((peers,)),
             dma((peers,)),
             dma,
             dma,
         ],
         compiler_params=pltpu.CompilerParams(
-            collective_id=0, has_side_effects=True, vmem_limit_bytes=48 * 2**20
+            collective_id=0, has_side_effects=True, vmem_limit_bytes=60 * 2**20
         ),
     )(pairs, conv_weight, qk_weight, v_weight, o_weight, upstream)
     return (

time: 78 us -> 70.1 us (0.90)
  the two profiles are of different devices: /device:TPU:11 before, /device:TPU:0 now
where the time goes in v2:
time: 70.1 us; the launch traced here: 69.8 us
  Pallas kernels  61 us (87%)
  local copies, waits for them, and re-layouts  8.18 us (12%)
    pallas_call x1, Pallas kernels, fused_body(): pl.pallas_call(functools.partial(fused_kernel, peers), out_shape=(jax.Sha...  61 us
    unnamed x2, local copies, waits for them, and re-layouts  4.69 us
    reshape x1, local copies, waits for them, and re-layouts, fused_body(): grad_fine.reshape(fine.shape)  1.74 us
    reshape x1, local copies, waits for them, and re-layouts, fused_body(): pairs = fine.reshape(2, n, 2 * chans)  1.74 us

profile of v2, /device:TPU:0, one launch (start us, length us, event | category | flops | bytes accessed | tf_op | source)
XLA Modules:
  0.0 69.8 jit_solution(9041352343102578473)
XLA Ops:
  0.6 1.7 %reshape.15.fine_hbm = bf16[2,128,512]{2,1,0:T(8,128)(2,1)} reshape(bf16[2,256,256]{2,1,0:T(8,128)(2,1)} %param.6) | data formatting | bytes 524288 | tf_op jit(solution)/shard_map/reshape | solution.py:545
  2.4 61.0 %shard_map.85 = (bf16[128,256]{1,0:T(8,128)(2,1)}, f32[9,256,256]{2,1,0:T(8,128)}, bf16[2,128,512]{2,1,0:T(8,128)(2,1)}) custom-call(bf16[2,128,512]{2,1,0:T(8,128)(2,1)} %reshape.15.fine_hbm, bf16[3,3,256,256]{3,2,1,0:T(8,128)(2,1)} %conv_hbm.1, bf16[2,256,128]{2,1,0:T(8,128)(2,1)} %qk_hbm.1, bf16[256,128]{1,0:T(8,128)(2,1)} %vw_hbm.1, ...), custom_call_target="tpu_custom_call" | custom-call | tf_op jit(solution)/shard_map/pallas_call | solution.py:548
  63.4 1.7 %reshape.17 = bf16[2,256,256]{2,1,0:T(8,128)(2,1)} reshape(bf16[2,128,512]{2,1,0:T(8,128)(2,1)} %get-tuple-element.8) | data formatting | bytes 524288 | tf_op jit(solution)/shard_map/reshape | solution.py:594
  65.1 1.5 %copy.11 = bf16[128,256]{1,0:T(8,128)(2,1)} copy(bf16[128,256]{1,0:T(8,128)(2,1)} %get-tuple-element.12) | data formatting | bytes 131072
  66.6 3.2 %copy.12 = f32[3,3,256,256]{3,2,1,0:T(8,128)} copy(f32[3,3,256,256]{3,2,1,0:T(8,128)} %bitcast.1) | data formatting | bytes 4718592

commit v3 on v2

--- a/solution.py
+++ b/solution.py
@@ -340,7 +340,7 @@
 
     def cols(ref, part):
         lines = pl.ds(part * chans, chans)
-        return lambda t: ref.at[lines, pl.ds(pl.multiple_of(t * n, n), n)]
+        return lambda t: ref.at[t, lines, :]
 
     mine = pl.ds(pl.multiple_of(me * n, n), n)
     loads[0].wait()
@@ -354,7 +354,7 @@
         device_id_type=pl.DeviceIdType.MESH,
     )
     halo.start()
-    fine_t[: 2 * chans, mine] = fine[0].T
+    fine_t[me, : 2 * chans, :] = fine[0].T
     parts = [Gather(cols(fine_t, p), me, peers, send, recv, i) for i, p in enumerate((0, 1, 3, 2))]
     hid_gather = Gather(rows(hid_all), me, peers, send, recv, 4)
     d_gather = Gather(rows(d_all), me, peers, send, recv, 5)
@@ -370,7 +370,7 @@
     mid, mid_late = conv_row(1, fine[0])
     low, low_late = conv_row(2, fine[1])
     dattended = mm(up[...], ow[...], NT).astype(jnp.bfloat16)
-    fine_t[2 * chans :, mine] = fine[1].T
+    fine_t[me, 2 * chans :, :] = fine[1].T
     halo.wait_recv()
     top_row = jnp.where(me == 0, jnp.zeros_like(above[...]), above[...])
     top, top_late = conv_row(0, top_row)
@@ -489,9 +489,9 @@
     grad_fine[0, :, chans:] = odd_mid.astype(jnp.bfloat16)
     even_low, odd_low = back_row(2, dhidden)
     dh_gather.across()
+    parts[3].across()
     dh_gather.over()
     parts[2].over()
-    parts[3].across()
     dh_gather.finish()
     below = dh_all[pl.ds(pl.multiple_of(lower * n, n), n), :]
     below = jnp.where(me == peers - 1, jnp.zeros_like(below), below)
@@ -505,14 +505,17 @@
     store(grad_fine, grad_fine_hbm)
     norm = 1.0 / math.sqrt(full)
 
+    def taps(features, count):
+        return jnp.concatenate([fine_t[t, features, :] for t in range(count)], axis=1)
+
     def finish_tap(a, b):
         source = dh_all if b else shift_all
         at = (2 if a != 1 else 0) * chans + (0 if b == 1 else chans)
         features = slice(at, at + chans)
         if a == 0:
-            part = mm(fine_t[features, : full - n], source[n:, :])
+            part = mm(taps(features, peers - 1), source[n:, :])
         else:
-            part = mm(fine_t[features, :], source[...])
+            part = mm(taps(features, peers), source[...])
         grad_conv[3 * a + b] = part * norm
         store(grad_conv.at[3 * a + b], grad_conv_hbm.at[3 * a + b])
 
@@ -573,7 +576,7 @@
             pltpu.VMEM((full, HD), jnp.bfloat16),
             pltpu.VMEM((full, chans), jnp.bfloat16),
             pltpu.VMEM((full, chans), jnp.bfloat16),
-            pltpu.VMEM((4 * chans, full), jnp.bfloat16),
+            pltpu.VMEM((peers, 4 * chans, n), jnp.bfloat16),
             pltpu.VMEM((peers, 2, 2 * n), jnp.float32),
             pltpu.VMEM((2 * n, full), jnp.float32),
             pltpu.VMEM((2 * n, full), jnp.float32),

time: 70.1 us -> 70 us (level)
  no operation moved by 1% of the time
where the time goes in v3:
time: 70 us; the launch traced here: 69.8 us
  Pallas kernels  61 us (87%)
  local copies, waits for them, and re-layouts  8.18 us (12%)
    pallas_call x1, Pallas kernels, fused_body(): pl.pallas_call(functools.partial(fused_kernel, peers), out_shape=(jax.Sha...  61 us
    unnamed x2, local copies, waits for them, and re-layouts  4.69 us
    reshape x1, local copies, waits for them, and re-layouts, fused_body(): grad_fine.reshape(fine.shape)  1.74 us
    reshape x1, local copies, waits for them, and re-layouts, fused_body(): pairs = fine.reshape(2, n, 2 * chans)  1.74 us

profile of v3, /device:TPU:0, one launch (start us, length us, event | category | flops | bytes accessed | tf_op | source)
XLA Modules:
  0.0 69.8 jit_solution(16143085090995621563)
XLA Ops:
  0.6 1.7 %reshape.15.fine_hbm = bf16[2,128,512]{2,1,0:T(8,128)(2,1)} reshape(bf16[2,256,256]{2,1,0:T(8,128)(2,1)} %param.6) | data formatting | bytes 524288 | tf_op jit(solution)/shard_map/reshape | solution.py:548
  2.4 61.0 %shard_map.85 = (bf16[128,256]{1,0:T(8,128)(2,1)}, f32[9,256,256]{2,1,0:T(8,128)}, bf16[2,128,512]{2,1,0:T(8,128)(2,1)}) custom-call(bf16[2,128,512]{2,1,0:T(8,128)(2,1)} %reshape.15.fine_hbm, bf16[3,3,256,256]{3,2,1,0:T(8,128)(2,1)} %conv_hbm.1, bf16[2,256,128]{2,1,0:T(8,128)(2,1)} %qk_hbm.1, bf16[256,128]{1,0:T(8,128)(2,1)} %vw_hbm.1, ...), custom_call_target="tpu_custom_call" | custom-call | tf_op jit(solution)/shard_map/pallas_call | solution.py:551
  63.3 1.7 %reshape.17 = bf16[2,256,256]{2,1,0:T(8,128)(2,1)} reshape(bf16[2,128,512]{2,1,0:T(8,128)(2,1)} %get-tuple-element.8) | data formatting | bytes 524288 | tf_op jit(solution)/shard_map/reshape | solution.py:597
  65.1 1.5 %copy.11 = bf16[128,256]{1,0:T(8,128)(2,1)} copy(bf16[128,256]{1,0:T(8,128)(2,1)} %get-tuple-element.12) | data formatting | bytes 131072
  66.5 3.2 %copy.12 = f32[3,3,256,256]{3,2,1,0:T(8,128)} copy(f32[3,3,256,256]{3,2,1,0:T(8,128)} %bitcast.1) | data formatting | bytes 4718592
